TPU v7x, 32 devices: a whole 2x2x4 slice. The times are simulated.
32 devices in a mesh: gx: 8 (over z, y), gy: 4 (over x, core).
Axes of the slice: x: 2, y: 2, z: 4, core: 2. Of those that a mesh axis runs over, the one named last changes fastest.
Arguments:
- psi: float32 [2, 256, 16, 1024], P(None, 'gx', None, 'gy'), may hold values from -6 to 6
- potential: float32 [256, 16, 1024], P('gx', None, 'gy'), may hold values from 0 to 4
Outputs:
- psi_half: float32 [2, 256, 16, 1024], P(None, 'gx', None, 'gy')
All inputs are finite; a program needn't handle non-finite values.
Results may differ from a plain program's by a relative error of at most 0.00005.
Values sent between devices are 32-bit elements; how exact they have to be, the bound alone decides.
A program may use at most 64 MiB of HBM per device.

v0:
```python
import jax
import jax.numpy as jnp
import numpy as np
from jax import lax
from jax.sharding import PartitionSpec as P

RYZ = 2


def with_halo(value, sides, width):
    for axis, dim in sides:
        peers, length = (lax.axis_size(axis), value.shape[dim])
        up = [(i, (i + 1) % peers) for i in range(peers - 1)]
        down = [(j, i) for i, j in up]
        last = lax.slice_in_dim(value, length - width, length, axis=dim)
        first = lax.slice_in_dim(value, 0, width, axis=dim)
        before = lax.ppermute(last, axis, up)
        after = lax.ppermute(first, axis, down)
        value = jnp.concatenate([before, value, after], axis=dim)
    return value


def cmul(left, right):
    return jnp.stack(
        [left[0] * right[0] - left[1] * right[1], left[0] * right[1] + left[1] * right[0]]
    )


def cinv(value):
    denom = value[0] * value[0] + value[1] * value[1]
    return jnp.stack([value[0] / denom, -value[1] / denom])


def local_inverse(cells):
    coef = 256.0 * cells * cells
    identity = np.eye(cells)
    cp_re_list = []
    cp_im_list = []
    dp_re_list = []
    dp_im_list = []
    cp_re = 0.0
    cp_im = 0.0
    dp_re = np.zeros(cells)
    dp_im = np.zeros(cells)
    for index in range(cells):
        piv_re = 1.0 - coef * cp_im
        piv_im = 2.0 * coef + coef * cp_re
        denom = piv_re * piv_re + piv_im * piv_im
        cp_re = -coef * piv_im / denom
        cp_im = -coef * piv_re / denom
        num_re = identity[index] - coef * dp_im
        num_im = coef * dp_re
        dp_re = (num_re * piv_re + num_im * piv_im) / denom
        dp_im = (num_im * piv_re - num_re * piv_im) / denom
        cp_re_list.append(cp_re)
        cp_im_list.append(cp_im)
        dp_re_list.append(dp_re)
        dp_im_list.append(dp_im)
    inv_re = np.zeros((cells, cells))
    inv_im = np.zeros((cells, cells))
    later_re = np.zeros(cells)
    later_im = np.zeros(cells)
    for index in range(cells - 1, -1, -1):
        next_re = dp_re_list[index] - (cp_re_list[index] * later_re - cp_im_list[index] * later_im)
        next_im = dp_im_list[index] - (cp_re_list[index] * later_im + cp_im_list[index] * later_re)
        later_re, later_im = (next_re, next_im)
        inv_re[index] = later_re
        inv_im[index] = later_im
    return (inv_re, inv_im, coef)


def shards(psi, potential):
    cells = psi.shape[1]
    count = lax.axis_size("gx")
    place = lax.axis_index("gx")
    inv_re, inv_im, coef = local_inverse(cells)
    upper_half = np.concatenate([inv_re, -inv_im], axis=1)
    lower_half = np.concatenate([inv_im, inv_re], axis=1)
    big = np.concatenate([upper_half, lower_half], axis=0).astype(np.float32)
    g_vec = jnp.asarray(np.stack([-coef * inv_im[:, 0], coef * inv_re[:, 0]]).astype(np.float32))
    h_vec = jnp.asarray(
        np.stack([-coef * inv_im[:, cells - 1], coef * inv_re[:, cells - 1]]).astype(np.float32)
    )
    s_val = g_vec[:, 0]
    t_val = g_vec[:, cells - 1]
    real_part, imag_part = (psi[0], psi[1])
    theta = 0.5 * (potential + real_part * real_part + imag_part * imag_part)
    cosine, sine = (jnp.cos(theta), jnp.sin(theta))
    turned = jnp.stack(
        [real_part * cosine + imag_part * sine, imag_part * cosine - real_part * sine]
    )
    padded = with_halo(turned, (("gy", 3),), 1)
    lap_y = padded[:, :, :, 2:] + padded[:, :, :, :-2] - 2.0 * turned
    z_padded = jnp.pad(turned, ((0, 0), (0, 0), (1, 1), (0, 0)))
    lap_z = z_padded[:, :, 2:] + z_padded[:, :, :-2] - 2.0 * turned
    side = RYZ * (lap_y + lap_z)
    rhs = jnp.stack([2.0 * turned[0] - side[1], 2.0 * turned[1] + side[0]])
    planes = rhs.shape[2]
    lines = rhs.shape[3]
    flat = rhs.reshape(2 * cells, planes * lines)
    local = jnp.dot(jnp.asarray(big), flat, precision=lax.Precision.HIGHEST).reshape(
        2, cells, planes, lines
    )
    first_val = local[:, 0]
    last_val = local[:, cells - 1]

    def advance(alpha, unused):
        q_val = cinv(
            jnp.stack(
                [
                    1.0 - (s_val[0] * alpha[0] - s_val[1] * alpha[1]),
                    -(s_val[0] * alpha[1] + s_val[1] * alpha[0]),
                ]
            )
        )
        aq_val = cmul(alpha, q_val)
        c_val = cmul(t_val, jnp.stack([1.0, 0.0]) + cmul(aq_val, s_val))
        mu_val = cmul(q_val, t_val)
        new_alpha = s_val + cmul(cmul(t_val, t_val), aq_val)
        return (new_alpha, (alpha, q_val, c_val, mu_val))

    unused, tables = lax.scan(advance, jnp.zeros((2,), jnp.float32), None, length=count)
    alphas, q_vals, c_vals, mu_vals = tables
    alpha_here = lax.dynamic_index_in_dim(alphas, place, 0, keepdims=False)
    q_here = lax.dynamic_index_in_dim(q_vals, place, 0, keepdims=False)
    mu_here = lax.dynamic_index_in_dim(mu_vals, place, 0, keepdims=False)
    fwd_term = last_val + cmul(cmul(t_val, cmul(alpha_here, q_here)), first_val)
    positions = jnp.arange(count, dtype=jnp.int32)

    def fwd_row(row, item):
        factor, index = item
        onehot = jnp.stack(
            [(positions == index).astype(jnp.float32), jnp.zeros((count,), jnp.float32)]
        )
        return (cmul(factor, row) + onehot, row)

    unused, fwd_rows = lax.scan(fwd_row, jnp.zeros((2, count), jnp.float32), (c_vals, positions))
    fwd_weights = lax.dynamic_index_in_dim(fwd_rows, place, 0, keepdims=False)
    piece = lax.all_gather(fwd_term[None], "gx", axis=0, tiled=True)
    weights = lax.slice_in_dim(fwd_weights, 0, piece.shape[0], axis=1)
    part_re = jnp.einsum(
        "k,kzy->zy", weights[0], piece[:, 0], precision=lax.Precision.HIGHEST
    ) - jnp.einsum("k,kzy->zy", weights[1], piece[:, 1], precision=lax.Precision.HIGHEST)
    part_im = jnp.einsum(
        "k,kzy->zy", weights[0], piece[:, 1], precision=lax.Precision.HIGHEST
    ) + jnp.einsum("k,kzy->zy", weights[1], piece[:, 0], precision=lax.Precision.HIGHEST)
    beta_prev = jnp.zeros_like(fwd_term) + jnp.stack([part_re, part_im])
    nu_here = cmul(q_here, first_val + cmul(s_val, beta_prev))

    def back_row(row, item):
        factor, index = item
        onehot = jnp.stack(
            [(positions == index).astype(jnp.float32), jnp.zeros((count,), jnp.float32)]
        )
        return (cmul(factor, row) + onehot, row)

    unused, back_rows = lax.scan(
        back_row, jnp.zeros((2, count), jnp.float32), (mu_vals, positions), reverse=True
    )
    back_weights = lax.dynamic_index_in_dim(back_rows, place, 0, keepdims=False)
    piece = lax.all_gather(nu_here[None], "gx", axis=0, tiled=True)
    weights = lax.slice_in_dim(back_weights, 0, piece.shape[0], axis=1)
    part_re = jnp.einsum(
        "k,kzy->zy", weights[0], piece[:, 0], precision=lax.Precision.HIGHEST
    ) - jnp.einsum("k,kzy->zy", weights[1], piece[:, 1], precision=lax.Precision.HIGHEST)
    part_im = jnp.einsum(
        "k,kzy->zy", weights[0], piece[:, 1], precision=lax.Precision.HIGHEST
    ) + jnp.einsum("k,kzy->zy", weights[1], piece[:, 0], precision=lax.Precision.HIGHEST)
    next_first = jnp.zeros_like(nu_here) + jnp.stack([part_re, part_im])
    first_here = cmul(mu_here, next_first) + nu_here
    edge_prev = cmul(alpha_here, first_here) + beta_prev
    from_left = cmul(g_vec[:, :, None, None], edge_prev[:, None])
    from_right = cmul(h_vec[:, :, None, None], next_first[:, None])
    return local + from_left + from_right - turned


def solution(mesh):
    return jax.shard_map(
        shards,
        mesh=mesh,
        in_specs=(P(None, "gx", None, "gy"), P("gx", None, "gy")),
        out_specs=P(None, "gx", None, "gy"),
        check_vma=False,
    )
```

profile of v0, /device:TPU:0, one launch (start us, length us, event | category | flops | bytes accessed | tf_op | source)
XLA Modules:
  0.0 309.6 jit_solution(17856614827695865240)
XLA Ops:
  0.0 3.6 %fusion.18 = (f32[32,16,256]{2,1,0:T(8,128)S(1)}, f32[32,16,256]{2,1,0:T(8,128)S(1)}) fusion(f32[2,32,16,256]{3,2,1,0:T(8,128)} %param.11, f32[32,16,256]{2,1,0:T(8,128)} %param.12), kind=kLoop, calls=%fused_computation.56 | loop fusion | flops 1441792 | bytes 2621440 | tf_op jit(solution)/shard_map/add | solution.py:90
  3.9 1.3 collective-permute-start
  5.2 3.8 %collective-permute-start.1 = (f32[2,32,16,1]{3,2,1,0:T(8,128)S(1)}, f32[2,32,16,1]{3,2,1,0:T(8,128)}, u32[]{:S(2)}, u32[]{:S(2)}) collective-permute-start(f32[2,32,16,1]{3,2,1,0:T(8,128)S(1)} %get-tuple-element.456), channel_id=1, source_target_pairs={{0,1},{1,2},{2,3},{4,5},{5,6},{6,7},{8,9},{9,10},{10,11},{12,13},{... | collective-permute-start | bytes 12296 | tf_op jit(solution)/shard_map/ppermute | solution.py:17
  9.7 162.3 %while.56 = (s32[]{:T(128)}, f32[2]{0:T(128)S(1)}, f32[8,2]{1,0:T(8,128)S(1)}, f32[8,2]{1,0:T(8,128)S(1)}, f32[8,2]{1,0:T(8,128)S(1)}, /*index=5*/f32[8,2]{1,0:T...) while((s32[]{:T(128)}, f32[2]{0:T(128)S(1)}, ...), condition=%wide.region_1.2_spmd.clone.clone, body=%wide.region_0.1_spmd.clone.clone.sunk | while | flops 63 | bytes 928 | solution.py:122
  10.3 0.7 fusion.85
  30.6 0.7 fusion.85
  50.9 0.7 fusion.85
  71.2 0.7 fusion.85
  91.5 0.7 fusion.85
  111.7 0.7 fusion.85
  132.0 0.7 fusion.85
  152.3 0.7 fusion.85
  172.0 0.6 fusion.66
  173.8 26.4 %while.55 = (s32[]{:T(128)}, f32[2,8]{1,0:T(2,128)S(1)}, f32[8,2,8]{2,1,0:T(2,128)S(1)}, f32[8,2]{1,0:T(8,128)S(1)}, s32[8]{0:T(128)S(1)}, /*index=5*/s32[]{:T(128)}, s32[]{:T(128)}) while((s32[]{:T(128)}, f32[2,8]{1,0:T(2,128)S(1)}, f32[8,2,8]{2,1,0:T(2,128)S(1)}, f32[8,2]{1,0:T(8,128)S(1)}, s32[8]{0:T(128)S(1)}, ...), condition=%wide.region_5.6_spmd.clone.clone, body=%wide.region_4.5_spmd.clone.clone.sunk | while | flops 123 | bytes 3535 | solution.py:137
  173.8 0.7 dynamic_slice.70
  174.5 0.7 compare_bitcast_fusion.5
  175.8 1.3 multiply_subtract_fusion.10
  177.1 0.7 dynamic_slice.70
  177.8 0.7 compare_bitcast_fusion.5
  179.1 1.3 multiply_subtract_fusion.10
  180.4 0.7 dynamic_slice.70
  181.1 0.7 compare_bitcast_fusion.5
  182.4 1.3 multiply_subtract_fusion.10
  183.7 0.7 dynamic_slice.70
  184.4 0.7 compare_bitcast_fusion.5
  185.7 1.3 multiply_subtract_fusion.10
  187.0 0.7 dynamic_slice.70
  187.7 0.7 compare_bitcast_fusion.5
  189.0 1.3 multiply_subtract_fusion.10
  190.4 0.7 dynamic_slice.70
  191.0 0.7 compare_bitcast_fusion.5
  192.3 1.3 multiply_subtract_fusion.10
  193.7 0.7 dynamic_slice.70
  194.3 0.7 compare_bitcast_fusion.5
  195.7 1.3 multiply_subtract_fusion.10
  197.0 0.7 dynamic_slice.70
  197.6 0.7 compare_bitcast_fusion.5
  199.0 1.3 multiply_subtract_fusion.10
  200.3 26.6 %while.54 = (s32[]{:T(128)}, f32[2,8]{1,0:T(2,128)S(1)}, f32[8,2,8]{2,1,0:T(2,128)S(1)}, f32[8,2]{1,0:T(8,128)S(1)}, s32[8]{0:T(128)S(1)}, /*index=5*/s32[]{:T(128)}, s32[]{:T(128)}, s32[]{:T(128)}) while((s32[]{:T(128)}, f32[2,8]{1,0:T(2,128)S(1)}, f32[8,2,8]{2,1,0:T(2,128)S(1)}, f32[8,2]{1,0:T(8,128)S(1)}, ...), condition=%wide.region_3.4_spmd.clone.clone, body=%wide.region_2.3_spmd.clone.clone.sunk | while | flops 124 | bytes 3555 | solution.py:157
  201.6 0.7 fusion.80
  202.3 1.3 multiply_subtract_fusion.9
  204.9 0.7 fusion.80
  205.6 1.3 multiply_subtract_fusion.9
  208.2 0.7 fusion.80
  208.9 1.3 multiply_subtract_fusion.9
  211.6 0.7 fusion.80
  212.2 1.3 multiply_subtract_fusion.9
  214.9 0.7 fusion.80
  215.6 1.3 multiply_subtract_fusion.9
  218.2 0.7 fusion.80
  218.9 1.3 multiply_subtract_fusion.9
  221.5 0.7 fusion.80
  222.2 1.3 multiply_subtract_fusion.9
  224.8 0.7 fusion.80
  225.5 1.3 multiply_subtract_fusion.9
  232.1 1.9 fusion.5
  235.1 1.0 fusion.68
  236.5 32.7 %all_gather.6 = f32[8,2,16,256]{3,2,1,0:T(8,128)S(1)} all-gather(f32[1,2,16,256]{3,2,1,0:T(8,128)S(1)} %fusion.37), channel_id=1, replica_groups=mesh['gx'=8,'gy'=4] {'gx'}, dimensions={0}, use_global_device_ids=true | all-gather | bytes 294912 | tf_op jit(solution)/shard_map/all_gather | solution.py:139
  270.6 1.3 multiply_subtract_fusion.5
  271.9 30.7 %all-gather = f32[16,16,256]{2,1,0:T(8,128)S(1)} all-gather(f32[2,16,256]{2,1,0:T(8,128)S(1)} %pad_maximum_fusion.6), channel_id=2, replica_groups=mesh['gx'=8,'gy'=4] {'gx'}, dimensions={0}, use_global_device_ids=true | all-gather | bytes 294912 | tf_op jit(solution)/shard_map/all_gather | solution.py:161
  303.9 1.2 subtract_bitcast_fusion
  305.1 1.2 add_bitcast_fusion
  306.4 1.4 multiply_subtract_fusion.4
  308.2 1.5 fusion.9
  (237 shorter events, 34.9 us)
Async XLA Ops:
  3.9 228.2 %collective-permute-start = (f32[2,32,16,1]{3,2,1,0:T(8,128)S(1)}, f32[2,32,16,1]{3,2,1,0:T(8,128)}, u32[]{:S(2)}, u32[]{:S(2)}) collective-permute-start(f32[2,32,16,1]{3,2,1,0:T(8,128)S(1)} %get-tuple-element.455), channel_id=1, source_target_pairs={{1,0},{2,1},{3,2},{5,4},{6,5},{7,6},{9,8},{10,9},{11,10},{13,12},{... | collective-permute-start | bytes 12296 | tf_op jit(solution)/shard_map/ppermute | solution.py:18
  5.2 226.9 %collective-permute-start.1 = (f32[2,32,16,1]{3,2,1,0:T(8,128)S(1)}, f32[2,32,16,1]{3,2,1,0:T(8,128)}, u32[]{:S(2)}, u32[]{:S(2)}) collective-permute-start(f32[2,32,16,1]{3,2,1,0:T(8,128)S(1)} %get-tuple-element.456), channel_id=1, source_target_pairs={{0,1},{1,2},{2,3},{4,5},{5,6},{6,7},{8,9},{9,10},{10,11},{12,13},{... | collective-permute-start | bytes 12296 | tf_op jit(solution)/shard_map/ppermute | solution.py:17
  9.0 0.7 copy-start
  9.0 0.7 copy-start.1
  9.0 0.7 copy-start.3
  234.4 0.8 copy-start.2
  270.6 37.2 %copy-start.6 = (f32[32]{0:T(128)S(1)}, f32[32]{0:T(128)}, u32[]{:S(2)}) copy-start(f32[32]{0:T(128)} %constant.154) | copy-start | bytes 388
  270.6 37.2 %copy-start.7 = (f32[32]{0:T(128)S(1)}, f32[32]{0:T(128)}, u32[]{:S(2)}) copy-start(f32[32]{0:T(128)} %constant.152) | copy-start | bytes 388
  302.9 5.0 %copy-start.4 = (f32[32]{0:T(128)S(1)}, f32[32]{0:T(128)}, u32[]{:S(2)}) copy-start(f32[32]{0:T(128)} %constant.150) | copy-start | bytes 388
  303.0 5.0 %copy-start.5 = (f32[32]{0:T(128)S(1)}, f32[32]{0:T(128)}, u32[]{:S(2)}) copy-start(f32[32]{0:T(128)} %constant.131) | copy-start | bytes 388
where the time goes:
time: 313 us; the launch traced here: 310 us
  loops' own time  144 us (46%)
  blocking collectives  63.5 us (20%)
  other arithmetic  47.9 us (15%)
  local copies, waits for them, and re-layouts  39.6 us (13%)
  between operations  5.62 us (2%)
  starting transfers between devices  5.13 us (2%)
  matrix products  3.47 us (1%)
    another operation x1, loops' own time, shards(): lax.scan(advance, jnp.zeros((2,), jnp.float32), None, length=count)  144 us
    all_gather x1, blocking collectives, shards(): piece = lax.all_gather(fwd_term[None], 'gx', axis=0, tiled=True)  32.7 us
    all_gather x1, blocking collectives, shards(): piece = lax.all_gather(nu_here[None], 'gx', axis=0, tiled=True)  30.7 us
    sub x21, other arithmetic, cmul(): left[0] * right[0] - left[1] * right[1]  23.7 us
    slice x18, local copies, waits for them, and re-layouts, cmul(): left[0] * right[0] - left[1] * right[1]  11.3 us
    dynamic_slice x32, local copies, waits for them, and re-layouts, shards(): lax.scan(fwd_row, jnp.zeros((2, count), jnp.float32), (c_vals, positions))  10.4 us
  transfers between devices with their start and end apart: 2, of which 0 were waited for; matrix products, arithmetic and copies ran while one was open for 23% of the time, Pallas kernels for 0%

commit v1 on v0

--- a/solution.py
+++ b/solution.py
@@ -136,7 +136,9 @@
 
     unused, fwd_rows = lax.scan(fwd_row, jnp.zeros((2, count), jnp.float32), (c_vals, positions))
     fwd_weights = lax.dynamic_index_in_dim(fwd_rows, place, 0, keepdims=False)
-    piece = lax.all_gather(fwd_term[None], "gx", axis=0, tiled=True)
+    piece = jnp.concatenate(
+        lax.all_to_all(jnp.stack([fwd_term[None]] * lax.axis_size("gx")), "gx", 0, 0), axis=0
+    )
     weights = lax.slice_in_dim(fwd_weights, 0, piece.shape[0], axis=1)
     part_re = jnp.einsum(
         "k,kzy->zy", weights[0], piece[:, 0], precision=lax.Precision.HIGHEST

time: 313 us -> 288 us (0.920)
  blocking collectives: 63.5 us -> 31.3 us
  starting transfers between devices: 5.13 us -> 12.4 us
    all_gather x1 -> x0, blocking collectives: 32.7 us -> none  [shards(): piece = lax.all_gather(fwd_term[None], 'gx', axis=0, tiled=True)]
    all_to_all x0 -> x1, starting transfers between devices: none -> 7.31 us  [shards(): lax.all_to_all(jnp.stack([fwd_term[None]] * lax.axis_size('gx')), 'gx', 0...]
    sub x21 -> x20, other arithmetic: 23.7 us -> 22.6 us  [cmul(): left[0] * right[0] - left[1] * right[1]]
  transfers between devices with their start and end apart: 2 -> 3, of which waited for: 0 -> 0; matrix products, arithmetic and copies ran while one was open for 23% -> 25% of each run, Pallas kernels for 0% -> 0%
where the time goes in v1:
time: 288 us; the launch traced here: 285 us
  loops' own time  146 us (51%)
  other arithmetic  46.5 us (16%)
  local copies, waits for them, and re-layouts  40.1 us (14%)
  blocking collectives  31.3 us (11%)
  starting transfers between devices  12.4 us (4%)
  between operations  5.37 us (2%)
  matrix products  3.47 us (1%)
    another operation x1, loops' own time, shards(): lax.scan(advance, jnp.zeros((2,), jnp.float32), None, length=count)  145 us
    all_gather x1, blocking collectives, shards(): piece = lax.all_gather(nu_here[None], 'gx', axis=0, tiled=True)  31.3 us
    sub x20, other arithmetic, cmul(): left[0] * right[0] - left[1] * right[1]  22.6 us
    slice x18, local copies, waits for them, and re-layouts, cmul(): left[0] * right[0] - left[1] * right[1]  10.9 us
    dynamic_slice x32, local copies, waits for them, and re-layouts, shards(): lax.scan(fwd_row, jnp.zeros((2, count), jnp.float32), (c_vals, positions))  9.76 us
    all_to_all x1, starting transfers between devices, shards(): lax.all_to_all(jnp.stack([fwd_term[None]] * lax.axis_size('gx')), 'gx', 0...  7.31 us
    slice x9, local copies, waits for them, and re-layouts, cmul(): left[1] * right[1]  5.8 us
  transfers between devices with their start and end apart: 3, of which 0 were waited for; matrix products, arithmetic and copies ran while one was open for 25% of the time, Pallas kernels for 0%

profile of v1, /device:TPU:0, one launch (start us, length us, event | category | flops | bytes accessed | tf_op | source)
XLA Modules:
  0.0 285.2 jit_solution(15327447686890287191)
XLA Ops:
  0.0 3.6 %fusion.18 = (f32[32,16,256]{2,1,0:T(8,128)S(1)}, f32[32,16,256]{2,1,0:T(8,128)S(1)}) fusion(f32[2,32,16,256]{3,2,1,0:T(8,128)} %param.11, f32[32,16,256]{2,1,0:T(8,128)} %param.12), kind=kLoop, calls=%fused_computation.56 | loop fusion | flops 1441792 | bytes 2621440 | tf_op jit(solution)/shard_map/add | solution.py:90
  3.9 1.3 collective-permute-start
  5.2 3.8 %collective-permute-start.1 = (f32[2,32,16,1]{3,2,1,0:T(8,128)S(1)}, f32[2,32,16,1]{3,2,1,0:T(8,128)}, u32[]{:S(2)}, u32[]{:S(2)}) collective-permute-start(f32[2,32,16,1]{3,2,1,0:T(8,128)S(1)} %get-tuple-element.456), channel_id=1, source_target_pairs={{0,1},{1,2},{2,3},{4,5},{5,6},{6,7},{8,9},{9,10},{10,11},{12,13},{... | collective-permute-start | bytes 12296 | tf_op jit(solution)/shard_map/ppermute | solution.py:17
  9.7 164.8 %while.56 = (s32[]{:T(128)}, f32[2]{0:T(128)S(1)}, f32[8,2]{1,0:T(8,128)S(1)}, f32[8,2]{1,0:T(8,128)S(1)}, f32[8,2]{1,0:T(8,128)S(1)}, /*index=5*/f32[8,2]{1,0:T...) while((s32[]{:T(128)}, f32[2]{0:T(128)S(1)}, ...), condition=%wide.region_1.2_spmd.clone.clone, body=%wide.region_0.1_spmd.clone.clone.sunk | while | flops 63 | bytes 928 | solution.py:122
  9.7 0.7 fusion.84
  10.3 0.7 fusion.85
  30.3 0.7 fusion.84
  30.9 0.7 fusion.85
  50.9 0.7 fusion.84
  51.6 0.7 fusion.85
  71.5 0.7 fusion.84
  72.2 0.7 fusion.85
  92.1 0.7 fusion.84
  92.8 0.7 fusion.85
  112.7 0.7 fusion.84
  113.4 0.7 fusion.85
  133.3 0.7 fusion.84
  134.0 0.7 fusion.85
  153.9 0.7 fusion.84
  154.6 0.7 fusion.85
  175.1 25.5 %while.54 = (s32[]{:T(128)}, f32[2,8]{1,0:T(2,128)S(1)}, f32[8,2,8]{2,1,0:T(2,128)S(1)}, f32[8,2]{1,0:T(8,128)S(1)}, s32[8]{0:T(128)S(1)}, /*index=5*/s32[]{:T(128)}, s32[]{:T(128)}, s32[]{:T(128)}) while((s32[]{:T(128)}, f32[2,8]{1,0:T(2,128)S(1)}, f32[8,2,8]{2,1,0:T(2,128)S(1)}, f32[8,2]{1,0:T(8,128)S(1)}, ...), condition=%wide.region_3.4_spmd.clone.clone, body=%wide.region_2.3_spmd.clone.clone.sunk | while | flops 124 | bytes 3555 | solution.py:159
  175.7 0.6 compare_bitcast_fusion.4
  177.0 1.3 multiply_subtract_fusion.8
  178.9 0.6 compare_bitcast_fusion.4
  180.2 1.3 multiply_subtract_fusion.8
  182.1 0.6 compare_bitcast_fusion.4
  183.4 1.3 multiply_subtract_fusion.8
  185.3 0.6 compare_bitcast_fusion.4
  186.6 1.3 multiply_subtract_fusion.8
  188.5 0.6 compare_bitcast_fusion.4
  189.8 1.3 multiply_subtract_fusion.8
  191.7 0.6 compare_bitcast_fusion.4
  193.0 1.3 multiply_subtract_fusion.8
  194.9 0.6 compare_bitcast_fusion.4
  196.2 1.3 multiply_subtract_fusion.8
  198.0 0.6 compare_bitcast_fusion.4
  199.3 1.3 multiply_subtract_fusion.8
  206.2 1.9 fusion.5
  209.2 1.0 fusion.68
  210.6 0.7 stack.197
  211.3 7.3 %all-to-all-start = ((f32[8,1,2,16,256]{4,3,2,1,0:T(8,128)}), f32[8,1,2,16,256]{4,3,2,1,0:T(8,128)S(1)}, u32[]{:S(2)}, u32[]{:S(2)}) async-start(f32[8,1,2,16,256]{4,3,2,1,0:T(8,128)} %stack.197), calls=%async_computation | async-start | bytes 524288 | tf_op jit(solution)/shard_map/all_to_all | solution.py:140
  218.7 25.0 %while.55 = (s32[]{:T(128)}, f32[2,8]{1,0:T(2,128)S(1)}, f32[8,2,8]{2,1,0:T(2,128)S(1)}, f32[8,2]{1,0:T(8,128)S(1)}, s32[8]{0:T(128)S(1)}, /*index=5*/s32[]{:T(128)}, s32[]{:T(128)}) while((s32[]{:T(128)}, f32[2,8]{1,0:T(2,128)S(1)}, f32[8,2,8]{2,1,0:T(2,128)S(1)}, f32[8,2]{1,0:T(8,128)S(1)}, s32[8]{0:T(128)S(1)}, ...), condition=%wide.region_5.6_spmd.clone.clone, body=%wide.region_4.5_spmd.clone.clone.sunk | while | flops 123 | bytes 3535 | solution.py:137
  219.3 0.6 compare_bitcast_fusion.5
  220.6 1.2 multiply_subtract_fusion.9
  222.4 0.6 compare_bitcast_fusion.5
  223.7 1.2 multiply_subtract_fusion.9
  225.6 0.6 compare_bitcast_fusion.5
  226.8 1.2 multiply_subtract_fusion.9
  228.7 0.6 compare_bitcast_fusion.5
  229.9 1.2 multiply_subtract_fusion.9
  231.8 0.6 compare_bitcast_fusion.5
  233.1 1.2 multiply_subtract_fusion.9
  234.9 0.6 compare_bitcast_fusion.5
  236.2 1.2 multiply_subtract_fusion.9
  238.1 0.6 compare_bitcast_fusion.5
  239.3 1.2 multiply_subtract_fusion.9
  241.2 0.6 compare_bitcast_fusion.5
  242.5 1.2 multiply_subtract_fusion.9
  245.7 1.3 multiply_subtract_fusion.5
  247.0 31.3 %all-gather = f32[16,16,256]{2,1,0:T(8,128)S(1)} all-gather(f32[2,16,256]{2,1,0:T(8,128)S(1)} %pad_maximum_fusion.6), channel_id=2, replica_groups=mesh['gx'=8,'gy'=4] {'gx'}, dimensions={0}, use_global_device_ids=true | all-gather | bytes 294912 | tf_op jit(solution)/shard_map/all_gather | solution.py:163
  279.6 1.2 subtract_bitcast_fusion
  280.8 1.2 add_bitcast_fusion
  282.0 1.2 multiply_subtract_fusion.4
  283.7 1.5 fusion.9
  (238 shorter events, 35.7 us)
Async XLA Ops:
  3.9 202.3 %collective-permute-start = (f32[2,32,16,1]{3,2,1,0:T(8,128)S(1)}, f32[2,32,16,1]{3,2,1,0:T(8,128)}, u32[]{:S(2)}, u32[]{:S(2)}) collective-permute-start(f32[2,32,16,1]{3,2,1,0:T(8,128)S(1)} %get-tuple-element.455), channel_id=1, source_target_pairs={{1,0},{2,1},{3,2},{5,4},{6,5},{7,6},{9,8},{10,9},{11,10},{13,12},{... | collective-permute-start | bytes 12296 | tf_op jit(solution)/shard_map/ppermute | solution.py:18
  5.2 201.0 %collective-permute-start.1 = (f32[2,32,16,1]{3,2,1,0:T(8,128)S(1)}, f32[2,32,16,1]{3,2,1,0:T(8,128)}, u32[]{:S(2)}, u32[]{:S(2)}) collective-permute-start(f32[2,32,16,1]{3,2,1,0:T(8,128)S(1)} %get-tuple-element.456), channel_id=1, source_target_pairs={{0,1},{1,2},{2,3},{4,5},{5,6},{6,7},{8,9},{9,10},{10,11},{12,13},{... | collective-permute-start | bytes 12296 | tf_op jit(solution)/shard_map/ppermute | solution.py:17
  9.0 0.7 copy-start
  9.0 0.7 copy-start.1
  9.0 0.7 copy-start.3
  208.5 0.8 copy-start.2
  211.3 33.0 %all-to-all-start = ((f32[8,1,2,16,256]{4,3,2,1,0:T(8,128)}), f32[8,1,2,16,256]{4,3,2,1,0:T(8,128)S(1)}, u32[]{:S(2)}, u32[]{:S(2)}) async-start(f32[8,1,2,16,256]{4,3,2,1,0:T(8,128)} %stack.197), calls=%async_computation | async-start | bytes 524288 | tf_op jit(solution)/shard_map/all_to_all | solution.py:140
  245.6 37.6 %copy-start.6 = (f32[32]{0:T(128)S(1)}, f32[32]{0:T(128)}, u32[]{:S(2)}) copy-start(f32[32]{0:T(128)} %constant.154) | copy-start | bytes 388
  245.7 37.6 %copy-start.7 = (f32[32]{0:T(128)S(1)}, f32[32]{0:T(128)}, u32[]{:S(2)}) copy-start(f32[32]{0:T(128)} %constant.152) | copy-start | bytes 388
  278.6 4.9 %copy-start.4 = (f32[32]{0:T(128)S(1)}, f32[32]{0:T(128)}, u32[]{:S(2)}) copy-start(f32[32]{0:T(128)} %constant.150) | copy-start | bytes 388
  278.6 4.9 %copy-start.5 = (f32[32]{0:T(128)S(1)}, f32[32]{0:T(128)}, u32[]{:S(2)}) copy-start(f32[32]{0:T(128)} %constant.131) | copy-start | bytes 388
